TPU v7x, 32 devices: a whole 2x2x4 slice. The times are simulated.
32 devices in a mesh: dp: 16 (over z, y, core), tensor: 2 (over x).
Axes of the slice: x: 2, y: 2, z: 4, core: 2. Of those that a mesh axis runs over, the one named last changes fastest.
Arguments:
- block_input: bfloat16 [16384, 768], P('dp'), may hold values from -6 to 6
- first_gain: float32 [768], replicated, may hold values from 0.5 to 1.5
- first_shift: float32 [768], replicated, may hold values from -1.2 to 1.2
- qkv_weight: bfloat16 [3, 768, 768], P(None, None, 'tensor'), may hold values from -0.21875 to 0.21875
- qv_bias: float32 [2, 768], P(None, 'tensor'), may hold values from -0.6 to 0.6
- proj_weight: bfloat16 [768, 768], P('tensor'), may hold values from -12 to 12
- proj_bias: float32 [768], replicated, may hold values from -6 to 6
- second_gain: float32 [768], replicated, may hold values from 0.5 to 1.5
- second_shift: float32 [768], replicated, may hold values from -1.2 to 1.2
- fc_weight: bfloat16 [768, 3072], P(None, 'tensor'), may hold values from -0.21875 to 0.21875
- fc_bias: float32 [3072], P('tensor'), may hold values from -3 to 3
- out_weight: bfloat16 [3072, 768], P('tensor'), may hold values from -0.75 to 0.75
- out_bias: float32 [768], replicated, may hold values from -6 to 6
- cotangent: bfloat16 [16384, 768], P('dp'), may hold values from -6 to 6
- lengths: int32 [16], P('dp'), may hold values from 256 to 1024, as said below
Outputs:
- block_output: bfloat16 [16384, 768], P('dp')
- grad_input: float32 [16384, 768], P('dp')
- grad_first_gain: float32 [768], replicated
- grad_first_shift: float32 [768], replicated
- grad_qkv_weight: float32 [3, 768, 768], P(None, 'dp', 'tensor')
- grad_qv_bias: float32 [2, 768], P(None, 'tensor')
- grad_proj_weight: float32 [768, 768], P('tensor', 'dp')
- grad_proj_bias: float32 [768], replicated
- grad_second_gain: float32 [768], replicated
- grad_second_shift: float32 [768], replicated
- grad_fc_weight: float32 [768, 3072], P('dp', 'tensor')
- grad_fc_bias: float32 [3072], P('tensor')
- grad_out_weight: float32 [3072, 768], P('tensor', 'dp')
- grad_out_bias: float32 [768], replicated
Inputs may be any that keep to these rules, and one draw needn't show every extreme that they name: Sequence s has its valid tokens in its first lengths[s] slots of 1024, padding after them; some sequence is full.
All inputs are finite; a program needn't handle non-finite values.
Results may differ from a plain program's by a relative error of at most 0.015.
Values may be sent and summed in bfloat16 or wider, within the bound.
No kernel may reach another device: no remote copies, remote signals or barrier semaphores. Data moves between devices by JAX's collectives and lax.ppermute only.
A program may use at most 192 MiB of HBM per device.

v0:
```python
import jax
import jax.numpy as jnp
from jax import lax
from jax.sharding import PartitionSpec as P

HEADS = 12


epsilon = 1e-05
branch_scale = 48 ** (-0.5)
gelu_coef = 0.7978845608028654
cubic_coef = 0.044715
masked_fill = -1000000000.0


def norm_parts(values):
    row_mean = jnp.mean(values, -1, keepdims=True)
    centered = values - row_mean
    inverse = lax.rsqrt(jnp.mean(centered * centered, -1, keepdims=True) + epsilon)
    return (centered * inverse, inverse)


def norm_back(grad_out, normed, inverse, gain_vec):
    scaled = grad_out * gain_vec
    inner_part = (
        scaled
        - jnp.mean(scaled, -1, keepdims=True)
        - normed * jnp.mean(scaled * normed, -1, keepdims=True)
    )
    return inverse * inner_part


def gelu_parts(hidden):
    tanh_part = jnp.tanh(gelu_coef * (hidden + cubic_coef * hidden * hidden * hidden))
    gelu_value = 0.5 * hidden * (1.0 + tanh_part)
    gelu_slope = 0.5 * (1.0 + tanh_part) + 0.5 * hidden * (
        1.0 - tanh_part * tanh_part
    ) * gelu_coef * (1.0 + 3.0 * cubic_coef * hidden * hidden)
    return (gelu_value, gelu_slope)


def masked_scores(queries, keys_low, seq_length, score_scale):
    raw = (
        jnp.einsum("qhd,khd->hqk", queries, keys_low, preferred_element_type=jnp.float32)
        * score_scale
    )
    positions = jnp.arange(queries.shape[0])
    allowed = (positions[:, None] >= positions[None, :]) & (positions[None, :] < seq_length)
    return jnp.where(allowed[None], raw, masked_fill)


def local(
    block_input,
    first_gain,
    first_shift,
    qkv_weight,
    qv_bias,
    proj_weight,
    proj_bias,
    second_gain,
    second_shift,
    fc_weight,
    fc_bias,
    out_weight,
    out_bias,
    cotangent,
    lengths,
):
    seq_count = lengths.shape[0]
    row_count = block_input.shape[0]
    seq_slots = row_count // seq_count
    local_width = qkv_weight.shape[2]
    local_heads = HEADS // lax.axis_size("tensor")
    head_size = local_width // local_heads
    score_scale = head_size ** (-0.5)
    head_shape = (seq_count, seq_slots, local_heads, head_size)
    resid = block_input.astype(jnp.float32)
    normed1, inverse1 = norm_parts(resid)
    a_low = (normed1 * first_gain + first_shift).astype(jnp.bfloat16)
    projected = jnp.einsum("td,kde->kte", a_low, qkv_weight, preferred_element_type=jnp.float32)
    queries = (projected[0] + qv_bias[0]).astype(jnp.bfloat16).reshape(head_shape)
    keys_low = projected[1].astype(jnp.bfloat16).reshape(head_shape)
    values_low = (projected[2] + qv_bias[1]).astype(jnp.bfloat16).reshape(head_shape)

    def attend(member):
        seq_queries, seq_keys, seq_values, seq_length = member
        scores = masked_scores(seq_queries, seq_keys, seq_length, score_scale)
        row_max = jnp.max(scores, -1, keepdims=True)
        expo = jnp.exp(scores - row_max)
        row_total = jnp.sum(expo, -1, keepdims=True)
        prob_low = (expo / row_total).astype(jnp.bfloat16)
        context = jnp.einsum(
            "hqk,khd->qhd", prob_low, seq_values, preferred_element_type=jnp.float32
        )
        return (context, row_max + jnp.log(row_total))

    context, log_totals = lax.map(attend, (queries, keys_low, values_low, lengths))
    context_low = context.reshape(row_count, local_width).astype(jnp.bfloat16)
    attn_part = jnp.dot(context_low, proj_weight, preferred_element_type=jnp.float32)
    attn_sum = lax.psum(attn_part.astype(jnp.bfloat16), "tensor").astype(jnp.float32)
    middle = resid + branch_scale * (attn_sum + proj_bias)
    normed2, inverse2 = norm_parts(middle)
    c_low = (normed2 * second_gain + second_shift).astype(jnp.bfloat16)
    hidden = jnp.dot(c_low, fc_weight, preferred_element_type=jnp.float32) + fc_bias
    activation, gelu_slope = gelu_parts(hidden)
    act_low = activation.astype(jnp.bfloat16)
    mlp_part = jnp.dot(act_low, out_weight, preferred_element_type=jnp.float32)
    mlp_sum = lax.psum(mlp_part.astype(jnp.bfloat16), "tensor").astype(jnp.float32)
    block_output = (middle + branch_scale * (mlp_sum + out_bias)).astype(jnp.bfloat16)
    positions = jnp.arange(seq_slots)
    valid_rows = (positions[None, :] < lengths[:, None]).astype(jnp.float32).reshape(row_count, 1)
    grad_top = cotangent.astype(jnp.float32) * valid_rows
    grad_out_bias = branch_scale * jnp.sum(grad_top, 0)
    grad_mlp = (branch_scale * grad_top).astype(jnp.bfloat16)
    grad_out_local = jnp.einsum("tf,td->fd", act_low, grad_mlp, preferred_element_type=jnp.float32)
    grad_act = jnp.einsum("td,fd->tf", grad_mlp, out_weight, preferred_element_type=jnp.float32)
    grad_hidden = (grad_act * gelu_slope).astype(jnp.bfloat16)
    grad_fc_bias = jnp.sum(grad_hidden.astype(jnp.float32), 0)
    grad_fc_local = jnp.einsum("td,tf->df", c_low, grad_hidden, preferred_element_type=jnp.float32)
    grad_c_part = jnp.einsum(
        "tf,df->td", grad_hidden, fc_weight, preferred_element_type=jnp.float32
    )
    grad_c = lax.psum(grad_c_part.astype(jnp.bfloat16), "tensor").astype(jnp.float32)
    grad_second_gain = jnp.sum(grad_c * normed2, 0)
    grad_second_shift = jnp.sum(grad_c, 0)
    grad_middle = grad_top + norm_back(grad_c, normed2, inverse2, second_gain)
    grad_proj_bias = branch_scale * jnp.sum(grad_middle, 0)
    grad_attn = (branch_scale * grad_middle).astype(jnp.bfloat16)
    grad_proj_local = jnp.einsum(
        "te,td->ed", context_low, grad_attn, preferred_element_type=jnp.float32
    )
    grad_context = (
        jnp.einsum("td,ed->te", grad_attn, proj_weight, preferred_element_type=jnp.float32)
        .astype(jnp.bfloat16)
        .reshape(head_shape)
    )

    def attend_back(member):
        seq_queries, seq_keys, seq_values, seq_grad, seq_logs, seq_length = member
        scores = masked_scores(seq_queries, seq_keys, seq_length, score_scale)
        attn_prob = jnp.exp(scores - seq_logs)
        grad_values = jnp.einsum(
            "hqk,qhd->khd",
            attn_prob.astype(jnp.bfloat16),
            seq_grad,
            preferred_element_type=jnp.float32,
        )
        grad_prob = jnp.einsum(
            "qhd,khd->hqk", seq_grad, seq_values, preferred_element_type=jnp.float32
        )
        grad_scores = (
            attn_prob * (grad_prob - jnp.sum(attn_prob * grad_prob, -1, keepdims=True))
        ).astype(jnp.bfloat16)
        grad_queries = (
            jnp.einsum("hqk,khd->qhd", grad_scores, seq_keys, preferred_element_type=jnp.float32)
            * score_scale
        )
        grad_keys = (
            jnp.einsum("hqk,qhd->khd", grad_scores, seq_queries, preferred_element_type=jnp.float32)
            * score_scale
        )
        return (grad_queries, grad_keys, grad_values)

    grad_queries, grad_keys, grad_values = lax.map(
        attend_back, (queries, keys_low, values_low, grad_context, log_totals, lengths)
    )
    grad_stack = jnp.stack(
        [
            grad_queries.reshape(row_count, local_width),
            grad_keys.reshape(row_count, local_width),
            grad_values.reshape(row_count, local_width),
        ]
    ).astype(jnp.bfloat16)
    grad_qv_bias = jnp.stack(
        [
            jnp.sum(grad_stack[0].astype(jnp.float32), 0),
            jnp.sum(grad_stack[2].astype(jnp.float32), 0),
        ]
    )
    grad_qkv_local = jnp.einsum(
        "td,kte->kde", a_low, grad_stack, preferred_element_type=jnp.float32
    )
    grad_a_part = jnp.einsum(
        "kte,kde->td", grad_stack, qkv_weight, preferred_element_type=jnp.float32
    )
    grad_a = lax.psum(grad_a_part.astype(jnp.bfloat16), "tensor").astype(jnp.float32)
    grad_first_gain = jnp.sum(grad_a * normed1, 0)
    grad_first_shift = jnp.sum(grad_a, 0)
    grad_input = grad_middle + norm_back(grad_a, normed1, inverse1, first_gain)
    grad_qkv_weight, grad_proj_weight, grad_fc_weight, grad_out_weight = (
        lax.psum_scatter(grad_qkv_local, "dp", scatter_dimension=1, tiled=True),
        lax.psum_scatter(grad_proj_local, "dp", scatter_dimension=1, tiled=True),
        lax.psum_scatter(grad_fc_local, "dp", scatter_dimension=0, tiled=True),
        lax.psum_scatter(grad_out_local, "dp", scatter_dimension=1, tiled=True),
    )
    (
        grad_first_gain,
        grad_first_shift,
        grad_qv_bias,
        grad_proj_bias,
        grad_second_gain,
        grad_second_shift,
        grad_fc_bias,
        grad_out_bias,
    ) = lax.psum(
        (
            grad_first_gain,
            grad_first_shift,
            grad_qv_bias,
            grad_proj_bias,
            grad_second_gain,
            grad_second_shift,
            grad_fc_bias,
            grad_out_bias,
        ),
        "dp",
    )
    return (
        block_output,
        grad_input,
        grad_first_gain,
        grad_first_shift,
        grad_qkv_weight,
        grad_qv_bias,
        grad_proj_weight,
        grad_proj_bias,
        grad_second_gain,
        grad_second_shift,
        grad_fc_weight,
        grad_fc_bias,
        grad_out_weight,
        grad_out_bias,
    )


def solution(mesh):
    placed = (
        P("dp", None),
        P(),
        P(),
        P(None, None, "tensor"),
        P(None, "tensor"),
        P("tensor", None),
        P(),
        P(),
        P(),
        P(None, "tensor"),
        P("tensor"),
        P("tensor", None),
        P(),
        P("dp", None),
        P("dp"),
    )
    return jax.shard_map(
        local,
        mesh=mesh,
        in_specs=placed,
        out_specs=(
            P("dp", None),
            P("dp", None),
            P(),
            P(),
            P(None, "dp", "tensor"),
            P(None, "tensor"),
            P("tensor", "dp"),
            P(),
            P(),
            P(),
            P("dp", "tensor"),
            P("tensor"),
            P("tensor", "dp"),
            P(),
        ),
        check_vma=False,
    )
```

profile of v0, /device:TPU:0, one launch (start us, length us, event | category | flops | bytes accessed | tf_op | source)
XLA Modules:
  0.0 711.4 jit_solution(10734078792318329568)
XLA Ops:
  11.2 3.9 convolution_bitcast_fusion
  18.4 12.0 %fusion.61 = (f32[6,1024]{1,0:T(8,128)S(1)}, f32[6,1024,1024]{1,2,0:T(8,128)}) fusion(bf16[1024,6,64]{0,2,1:T(8,128)(2,1)S(1)} %bitcast.52, f32[1024,6,64]{0,2,1:T(8,128)} %bitcast.50, f32[6,64]{1,0:T(8,128)S(1)} %add.154, pred[1024,1024]{0,1:T(8,128)(4,1)S(1)} %fusion.19), kind=kOutput, calls=%fused_computation.113 | convolution fusion | flops 824961024 | bytes 28599808 | tf_op jit(solution)/shard_map/while/body/eval_jaxpr/qhd,khd->hqk/dot_general | solution.py:44
  30.4 10.3 %fusion = f32[6,1024]{1,0:T(8,128)S(1)} fusion(f32[6,1024,1024]{1,2,0:T(8,128)} %get-tuple-element.121, f32[6,1024]{1,0:T(8,128)S(1)} %get-tuple-element.120), kind=kLoop, calls=%fused_computation.6 | loop fusion | flops 12576768 | bytes 25214976 | tf_op jit(solution)/shard_map/while/body/eval_jaxpr/reduce_sum | solution.py:90
  40.7 10.7 %fusion.42 = bf16[6,64,1024]{2,1,0:T(8,128)(2,1)S(1)} fusion(f32[6,1024,1024]{1,2,0:T(8,128)} %get-tuple-element.121, f32[6,1024]{1,0:T(8,128)S(1)} %fusion, f32[6,1024]{1,0:T(8,128)S(1)} %get-tuple-element.120, f32[1024,6,64]{0,2,1:T(8,128)S(1)} %bitcast.59, f32[6,64]{1,0:T(8,128)S(1)} %add.151), kind=kOutput, calls=%fused_computation.81 | convolution fusion | flops 825360384 | bytes 27575808 | tf_op jit(solution)/shard_map/while/body/eval_jaxpr/hqk,khd->qhd/dot_general | solution.py:92
  54.8 54.0 %all-reduce.8.cloned.1.call-done = bf16[1024,768]{1,0:T(8,128)(2,1)} async-done(((bf16[1024,768]{1,0:T(8,128)(2,1)}), bf16[1024,768]{1,0:T(8,128)(2,1)}) %all-reduce.8.cloned.1.call-update) | async-done | bytes 1572880 | tf_op jit(solution)/shard_map/psum | solution.py:100
  108.9 2.7 fusion.55
  112.7 3.0 fusion.57
  115.8 6.2 convert_reduce_fusion
  123.7 3.7 convolution_convert_fusion.1
  127.8 51.3 %all-reduce.10.cloned.1.call-done = bf16[1024,768]{1,0:T(8,128)(2,1)} async-done(((bf16[1024,768]{1,0:T(8,128)(2,1)}), bf16[1024,768]{1,0:T(8,128)(2,1)}) %all-reduce.10.cloned.1.call-update) | async-done | bytes 1572880 | tf_op jit(solution)/shard_map/psum | solution.py:123
  179.1 4.3 fusion.35
  183.5 3.7 fusion.58
  190.6 13.2 %fusion.39 = bf16[6,64,1024]{2,1,0:T(8,128)(2,1)} fusion(bf16[1024,6,64]{0,2,1:T(8,128)(2,1)} %bitcast.56, f32[6,1024,1024]{1,2,0:T(8,128)} %get-tuple-element.121, f32[6,1024]{1,0:T(8,128)S(1)} %log_add_fusion), kind=kOutput, calls=%fused_computation.80 | convolution fusion | flops 818282496 | bytes 26763264 | tf_op jit(solution)/shard_map/while/body/eval_jaxpr/hqk,qhd->khd/dot_general | solution.py:142
  203.9 16.6 %multiply_reduce_fusion = (f32[6,1024]{1,0:T(8,128)S(1)}, f32[6,1024,1024]{1,2,0:T(8,128)}) fusion(f32[6,1024,1024]{1,2,0:T(8,128)} %get-tuple-element.121, f32[6,1024]{1,0:T(8,128)S(1)} %log_add_fusion, bf16[1024,6,64]{0,2,1:T(8,128)(2,1)} %bitcast.57, f32[1024,6,64]{0,2,1:T(8,128)} %bitcast.58, f32[6,64]{1,0:T(8,128)S(1)} %add.151), kind=kOutput, calls=%fused_computation.1 | convolution fusion | flops 824961024 | bytes 52741632 | tf_op jit(solution)/shard_map/while/body/eval_jaxpr/qhd,khd->hqk/dot_general | solution.py:148
  220.4 21.7 %multiply_convert_fusion = bf16[6,1024,1024]{1,2,0:T(8,128)(2,1)} fusion(f32[6,1024,1024]{1,2,0:T(8,128)} %get-tuple-element.123, f32[6,1024,1024]{1,2,0:T(8,128)} %get-tuple-element.121, f32[6,1024]{1,0:T(8,128)S(1)} %get-tuple-element.122, f32[6,1024]{1,0:T(8,128)S(1)} %log_add_fusion), kind=kLoop, calls=%fused_computation | loop fusion | flops 25165824 | bytes 62963712 | tf_op jit(solution)/shard_map/while/body/eval_jaxpr/convert_element_type | solution.py:153
  242.1 9.4 %multiply_convert_fusion.4 = bf16[6,64,1024]{2,1,0:T(8,128)(2,1)} fusion(bf16[6,1024,1024]{1,2,0:T(8,128)(2,1)} %multiply_convert_fusion, f32[1024,6,64]{0,2,1:T(8,128)S(1)} %bitcast.51, f32[6,64]{1,0:T(8,128)S(1)} %add.154), kind=kOutput, calls=%fused_computation.75 | convolution fusion | flops 806879232 | bytes 14943744 | tf_op jit(solution)/shard_map/while/body/eval_jaxpr/hqk,qhd->khd/dot_general | solution.py:159
  251.5 7.8 %multiply_convert_fusion.5 = bf16[6,64,1024]{2,1,0:T(8,128)(2,1)} fusion(bf16[1024,6,64]{0,2,1:T(8,128)(2,1)S(1)} %bitcast.53, bf16[6,1024,1024]{1,2,0:T(8,128)(2,1)} %multiply_convert_fusion), kind=kOutput, calls=%fused_computation.76 | convolution fusion | flops 806092800 | bytes 14155776 | tf_op jit(solution)/shard_map/while/body/eval_jaxpr/hqk,khd->qhd/dot_general | solution.py:155
  259.3 2.4 copy.46
  265.2 6.3 convolution_bitcast_fusion.1
  271.5 6.2 copy.48
  278.0 8.0 %convolution_convert_fusion.2 = bf16[1024,768]{1,0:T(8,128)(2,1)} fusion(bf16[1536,768]{1,0:T(8,128)(2,1)S(1)} %copy-done, f32[1024,1536]{1,0:T(8,128)} %copy-done.32, f32[1536]{0:T(1024)S(1)} %copy-done.27), kind=kOutput, calls=%fused_computation.70 | convolution fusion | flops 2432434176 | bytes 10229760 | tf_op jit(solution)/shard_map/dot_general | solution.py:107
  286.1 3.5 bitcast_convert_fusion
  290.7 4.0 fusion.43
  294.7 9.0 %fusion.44 = f32[1536,768]{0,1:T(8,128)} fusion(bf16[1024,768]{1,0:T(8,128)(2,1)} %param.28, f32[1024]{0:T(1024)S(1)} %fusion.48, f32[1024,1536]{1,0:T(8,128)} %copy-done.32, f32[1536]{0:T(1024)S(1)} %copy-done.27), kind=kOutput, calls=%fused_computation.83 | convolution fusion | flops 2434793472 | bytes 12593152 | tf_op jit(solution)/shard_map/tf,td->fd/dot_general | solution.py:115
  304.0 8.1 %fusion.56 = f32[768,1536]{1,0:T(8,128)} fusion(bf16[1024,1536]{1,0:T(8,128)(2,1)} %copy-done.31, f32[768]{0:T(1024)S(1)} %copy-done.29, f32[768]{0:T(1024)S(1)} %copy-done.21, f32[1024]{0:T(1024)S(1)} %add_rsqrt_fusion, f32[1024]{0:T(1024)S(1)} %broadcast_multiply_fusion.6, f32[768]{0:T(1024)S(1)} %copy-done.20, ...), kind=kOutput, calls=%fused_computation.109 | convolution fusion | flops 2423783424 | bytes 11027456 | tf_op jit(solution)/shard_map/td,tf->df/dot_general | solution.py:119
  315.6 79.3 %all-reduce.12.cloned.1.call-done = f32[3,768,384]{2,0,1:T(4,128)} async-done(((f32[3,768,384]{2,0,1:T(4,128)}), f32[3,768,384]{2,0,1:T(4,128)}) %all-reduce.12.cloned.1.call-update) | async-done | bytes 3538960
  396.6 86.7 %all-reduce.14.cloned.1.call-done = (bf16[1024,768]{1,0:T(8,128)(2,1)}, bf16[1024,768]{1,0:T(8,128)(2,1)}) async-done(((bf16[1024,768]{1,0:T(8,128)(2,1)}, bf16[1024,768]{1,0:T(8,128)(2,1)}), (bf16[1024,768]{1,0:T(8,128)(2,1)}, bf16[1024,768]{1,0:T(8,128)(2,1)})) %all-reduce.14.cloned.1.call-update) | async-done | bytes 3145744 | tf_op jit(solution)/shard_map/psum | solution.py:108
  483.4 3.0 fusion.36
  486.4 61.9 %all-reduce.1 = (f32[768]{0:T(1024)}, f32[768]{0:T(1024)}, f32[2,384]{1,0:T(2,128)}, f32[768]{0:T(1024)}, f32[768]{0:T(1024)}, /*index=5*/f32[768]{0:T(1024)}, f32[1536]{0:T(1024)}, f32[768]{0:T(1024)}) all-reduce(f32[768]{0:T(1024)S(1)} %get-tuple-element.95, ...), channel_id=1, replica_groups=mesh['dp'=16,'tensor'=2] {'dp'}, use_global_device_ids=true, to_apply=%region_16.17 | all-reduce | flops 6912 | bytes 55296 | tf_op jit(solution)/shard_map/psum | solution.py:205
  548.3 6.1 fusion.28
  554.4 70.9 %reduce-scatter.8.cloned.1.call-done = f32[1536,48]{0,1:T(8,128)} async-done(((f32[1536,768]{0,1:T(8,128)}), f32[1536,48]{0,1:T(8,128)}) %reduce-scatter.8.cloned.1.call-update) | async-done | bytes 294928 | tf_op jit(solution)/shard_map/reduce_scatter | solution.py:194
  625.3 79.0 %reduce-scatter.6.cloned.1.call-done = f32[48,1536]{1,0:T(8,128)} async-done(((f32[768,1536]{1,0:T(8,128)}), f32[48,1536]{1,0:T(8,128)}) %reduce-scatter.6.cloned.1.call-update) | async-done | bytes 294928 | tf_op jit(solution)/shard_map/reduce_scatter | solution.py:193
  (114 shorter events, 26.2 us)
Async XLA Ops:
  7.2 108.6 %copy-start = (bf16[1536,768]{1,0:T(8,128)(2,1)S(1)}, bf16[1536,768]{1,0:T(8,128)(2,1)}, u32[]{:S(2)}) copy-start(bf16[1536,768]{1,0:T(8,128)(2,1)} %param.26) | copy-start | bytes 7077892
  7.2 4.0 copy-start.22
  7.2 4.0 copy-start.28
  7.2 101.6 %all-reduce.8.cloned.1.call-start = ((), (), s32[]{:S(2)}) async-start(), calls=%async_computation.3 | async-start | bytes 3145728 | tf_op jit(solution)/shard_map/psum | solution.py:100
  7.3 3.9 copy-start.1
  30.4 10.3 %copy-start.11 = (f32[1,1024,384]{1,2,0:T(8,128)S(1)}, f32[1,1024,384]{1,2,0:T(8,128)}, u32[]{:S(2)}) copy-start(f32[1,1024,384]{1,2,0:T(8,128)} %get-tuple-element.115) | copy-start | bytes 4718596
  40.7 11.6 %copy-start.18 = (bf16[384,768]{1,0:T(8,128)(2,1)S(1)}, bf16[384,768]{1,0:T(8,128)(2,1)}, u32[]{:S(2)}) copy-start(bf16[384,768]{1,0:T(8,128)(2,1)} %param.20) | copy-start | bytes 1769476
  51.4 57.4 %copy-start.20 = (f32[768]{0:T(1024)S(1)}, f32[768]{0:T(1024)}, u32[]{:S(2)}) copy-start(f32[768]{0:T(1024)} %param.21) | copy-start | bytes 9220
  54.5 124.6 %all-reduce.10.cloned.1.call-start = ((), (), s32[]{:S(2)}) async-start(), calls=%async_computation.4 | async-start | bytes 3145728 | tf_op jit(solution)/shard_map/psum | solution.py:123
  54.8 57.9 %copy-start.21 = (f32[768]{0:T(1024)S(1)}, f32[768]{0:T(1024)}, u32[]{:S(2)}) copy-start(f32[768]{0:T(1024)} %param.22) | copy-start | bytes 9220
  54.8 57.9 %copy-start.29 = (f32[768]{0:T(1024)S(1)}, f32[768]{0:T(1024)}, u32[]{:S(2)}) copy-start(f32[768]{0:T(1024)} %param.23) | copy-start | bytes 9220
  108.8 2.8 copy-start.5
  108.8 3.8 copy-start.25
  112.7 3.1 copy-start.12
  112.7 3.1 copy-start.27
  115.8 6.2 copy-start.32
  127.5 267.4 %all-reduce.12.cloned.1.call-start = ((), (), s32[]{:S(2)}) async-start(), calls=%async_computation.8 | async-start | bytes 9437184
  179.1 4.4 copy-start.3
  179.1 4.4 copy-start.6
  179.1 4.4 copy-start.10
  183.5 5.4 copy-start.19
  220.4 21.7 %copy-start.7 = (f32[1,1024,384]{1,2,0:T(8,128)S(1)}, f32[1,1024,384]{1,2,0:T(8,128)}, u32[]{:S(2)}) copy-start(f32[1,1024,384]{1,2,0:T(8,128)} %get-tuple-element.116) | copy-start | bytes 4718596
  259.3 4.7 copy-start.9
  277.7 8.3 %copy-start.15 = (bf16[1,1024,384]{2,1,0:T(8,128)(2,1)S(1)}, bf16[1,1024,384]{2,1,0:T(8,128)(2,1)}, u32[]{:S(2)}) copy-start(bf16[1,1024,384]{2,1,0:T(8,128)(2,1)} %copy.46) | copy-start | bytes 2359300
  277.8 205.6 %all-reduce.14.cloned.1.call-start = ((), (), s32[]{:S(2)}) async-start(), calls=%async_computation.9 | async-start | bytes 6291456 | tf_op jit(solution)/shard_map/psum | solution.py:108
  278.0 8.1 %copy-start.16 = (bf16[1,1024,384]{2,1,0:T(8,128)(2,1)S(1)}, bf16[1,1024,384]{2,1,0:T(8,128)(2,1)}, u32[]{:S(2)}) copy-start(bf16[1,1024,384]{2,1,0:T(8,128)(2,1)} %copy.45) | copy-start | bytes 2359300
  278.0 8.1 %copy-start.17 = (bf16[1,1024,384]{2,1,0:T(8,128)(2,1)S(1)}, bf16[1,1024,384]{2,1,0:T(8,128)(2,1)}, u32[]{:S(2)}) copy-start(bf16[1,1024,384]{2,1,0:T(8,128)(2,1)} %copy.44) | copy-start | bytes 2359300
  278.0 8.0 %copy-start.26 = (bf16[3,768,384]{2,1,0:T(8,128)(2,1)S(1)}, bf16[3,768,384]{2,1,0:T(8,128)(2,1)}, u32[]{:S(2)}) copy-start(bf16[3,768,384]{2,1,0:T(8,128)(2,1)} %param.18) | copy-start | bytes 5308420
  289.5 264.8 %reduce-scatter.4.cloned.1.call-start = ((), (), s32[]{:S(2)}) async-start(), calls=%async_computation.5 | async-start | bytes 1253376 | tf_op jit(solution)/shard_map/reduce_scatter | solution.py:192
  294.6 330.7 %reduce-scatter.8.cloned.1.call-start = ((), (), s32[]{:S(2)}) async-start(), calls=%async_computation.7 | async-start | bytes 5013504 | tf_op jit(solution)/shard_map/reduce_scatter | solution.py:194
  303.8 400.6 %reduce-scatter.6.cloned.1.call-start = ((), (), s32[]{:S(2)}) async-start(), calls=%async_computation.6 | async-start | bytes 5013504 | tf_op jit(solution)/shard_map/reduce_scatter | solution.py:193
  312.2 236.1 %copy-start.23 = (f32[768]{0:T(1024)S(1)}, f32[768]{0:T(1024)}, u32[]{:S(2)}) copy-start(f32[768]{0:T(1024)} %param.27) | copy-start | bytes 9220
  (8 other events, 13.5 us)
Sparse Core Ops, SparseCore 0:
  54.6 54.1 all-reduce.7
  127.6 51.4 all-reduce.9
  277.9 117.0 all-reduce.11
  397.7 85.6 all-reduce.13
  487.8 57.9 reduce-scatter.3
  550.6 74.6 reduce-scatter.7
  629.7 74.5 reduce-scatter.5
where the time goes:
time: 720 us; the launch traced here: 711 us
  waiting for transfers between devices  421 us (58%)
  matrix products  129 us (18%)
  blocking collectives  61.9 us (9%)
  other arithmetic  58.6 us (8%)
  local copies, waits for them, and re-layouts  22.9 us (3%)
  between operations  16.2 us (2%)
    psum x1, waiting for transfers between devices, local(): lax.psum(mlp_part.astype(jnp.bfloat16), 'tensor').astype(jnp.float32)  86.7 us
    unnamed x8, waiting for transfers between devices  79.4 us
    reduce_scatter x1, waiting for transfers between devices, local(): lax.psum_scatter(grad_fc_local, 'dp', scatter_dimension=0, tiled=True)  79 us
    reduce_scatter x1, waiting for transfers between devices, local(): lax.psum_scatter(grad_out_local, 'dp', scatter_dimension=1, tiled=True)  70.9 us
    psum x1, blocking collectives, local(): lax.psum((grad_first_gain, grad_first_shift, grad_qv_bias, grad_proj_bias...  61.9 us
    psum x1, waiting for transfers between devices, local(): lax.psum(attn_part.astype(jnp.bfloat16), 'tensor').astype(jnp.float32)  54 us
    psum x1, waiting for transfers between devices, local(): lax.psum(grad_c_part.astype(jnp.bfloat16), 'tensor').astype(jnp.float32)  51.3 us
    convert_element_type x1, other arithmetic, attend_back(): grad_scores = (attn_prob * (grad_prob - jnp.sum(attn_prob * grad_prob, -1...  21.7 us
  transfers between devices with their start and end apart: 7, of which 6 were waited for; matrix products, arithmetic and copies ran while one was open for 6% of the time, Pallas kernels for 0%

commit v1 on v0

v1 whole, which is shorter than its diff:
```python
import functools

import jax
import jax.numpy as jnp
from jax import lax
from jax.experimental import pallas as pl
from jax.experimental.pallas import tpu as pltpu
from jax.sharding import PartitionSpec as P

HEADS = 12
EPSILON = 1e-05
BRANCH = 48 ** (-0.5)
GELU = 0.7978845608028654
CUBIC = 0.044715
FILL = -1e30
BF = jnp.bfloat16
F32 = jnp.float32
VMEM_LIMIT = 60 * 1024 * 1024
TILE = 256
ROWS = 512
HIDDEN = 512


def dot(left, right):
    return lax.dot_general(left, right, (((1,), (0,)), ((), ())), preferred_element_type=F32)


def dot_nt(left, right):
    return lax.dot_general(left, right, (((1,), (1,)), ((), ())), preferred_element_type=F32)


def norm_parts(values):
    row_mean = jnp.mean(values, -1, keepdims=True)
    centered = values - row_mean
    inverse = lax.rsqrt(jnp.mean(centered * centered, -1, keepdims=True) + EPSILON)
    return centered * inverse, inverse


def norm_back(grad_out, normed, inverse, gain):
    scaled = grad_out * gain
    inner = (
        scaled
        - jnp.mean(scaled, -1, keepdims=True)
        - normed * jnp.mean(scaled * normed, -1, keepdims=True)
    )
    return inverse * inner


def vmem():
    return pl.BlockSpec(memory_space=pltpu.VMEM)


def smem():
    return pl.BlockSpec(memory_space=pltpu.SMEM)


def anywhere():
    return pl.BlockSpec(memory_space=pl.ANY)


def call(body, name, outs, specs, scratch, flops, args):
    moved = sum(a.size * a.dtype.itemsize for a in args)
    moved += sum(o.size * o.dtype.itemsize for o in outs)
    return pl.pallas_call(
        body,
        name=name,
        out_shape=outs,
        in_specs=specs,
        out_specs=tuple(vmem() for _ in outs),
        scratch_shapes=scratch,
        compiler_params=pltpu.CompilerParams(vmem_limit_bytes=VMEM_LIMIT),
        cost_estimate=pl.CostEstimate(flops=flops, bytes_accessed=moved, transcendentals=0),
    )(*args)


def out(shape, dtype):
    return jax.ShapeDtypeStruct(shape, dtype)


def fetch_rows(pieces, target, turn, sems):
    count = len(pieces)
    copies = []
    for index, piece in enumerate(pieces):
        rows = piece.shape[-2]
        place = xor_index(index, turn) if count > 1 else 0
        start = pl.multiple_of(place * rows, 32) if count > 1 else 0
        where = pl.ds(start, rows)
        view = target.at[:, where, :] if len(target.shape) == 3 else target.at[where, :]
        copies.append(pltpu.make_async_copy(piece, view, sems.at[index]))
    return copies


def xor_index(index, turn):
    return jnp.bitwise_xor(jnp.int32(index), turn)


def forward_kernel(own, count, turn_ref, length_ref, source_ref, gain_ref, shift_ref, bias_ref, *rest):
    pieces, rest = rest[:count], rest[count:]
    if own:
        a_ref, at_ref, rest = rest[0], rest[1], rest[2:]
    else:
        a_ref = source_ref
    q_ref, k_ref, v_ref, ctx_ref, ctxt_ref, lse_ref, w_ref, vt_ref, aug_ref, sems = rest
    copies = fetch_rows(pieces, w_ref, turn_ref[0], sems)
    for copy in copies:
        copy.start()
    slots, width = q_ref.shape
    length = length_ref[0]
    if own:
        for start in range(0, slots, ROWS):
            rows = slice(start, start + ROWS)
            normed, _ = norm_parts(source_ref[rows, :].astype(F32))
            low = (normed * gain_ref[...] + shift_ref[...]).astype(BF)
            a_ref[rows, :] = low
            at_ref[:, rows] = low.T
    for copy in copies:
        copy.wait()
    for start in range(0, slots, ROWS):
        rows = slice(start, start + ROWS)
        low = a_ref[rows, :]
        q_ref[rows, :] = ((dot(low, w_ref[0]) + bias_ref[0:1, :]).astype(BF) * 0.125).astype(BF)
        k_ref[rows, :] = dot(low, w_ref[1]).astype(BF)
        values = (dot(low, w_ref[2]) + bias_ref[1:2, :]).astype(BF)
        v_ref[rows, :] = values
        vt_ref[:, rows] = values.T

    @pl.loop(0, width // 128)
    def _(pair):
        lanes = pl.ds(pl.multiple_of(pair * 128, 128), 128)
        lane_k = lax.broadcasted_iota(jnp.int32, (slots, 128), 1)
        pos_k = lax.broadcasted_iota(jnp.int32, (slots, 128), 0)
        bias = jnp.where(pos_k < length, 0.0, FILL)
        k_pair = k_ref[:, lanes].astype(F32)
        for half in (0, 1):
            bias_lane = 64 * (1 - half)
            aug_ref[half] = jnp.where(lane_k == bias_lane, bias, k_pair).astype(BF)
        lane_q = lax.broadcasted_iota(jnp.int32, (TILE, 128), 1)
        key_pos = lax.broadcasted_iota(jnp.int32, (TILE, TILE), 0)
        query_pos = lax.broadcasted_iota(jnp.int32, (TILE, TILE), 1)
        causal = jnp.where(key_pos <= query_pos, 0.0, FILL)
        for block in range(slots // TILE):
            extent = (block + 1) * TILE
            columns = slice(block * TILE, extent)
            q_pair = q_ref[columns, lanes].astype(F32)
            for half in (0, 1):
                bias_lane = 64 * (1 - half)
                q_aug = jnp.where(
                    lane_q // 64 == half, q_pair, jnp.where(lane_q == bias_lane, 1.0, 0.0)
                ).astype(BF)
                scores = dot_nt(aug_ref[half, :extent, :], q_aug)
                diagonal = scores[extent - TILE :] + causal
                row_max = jnp.max(diagonal, 0, keepdims=True)
                if block:
                    row_max = jnp.maximum(
                        row_max, jnp.max(scores[: extent - TILE], 0, keepdims=True)
                    )
                expo = jnp.exp(diagonal - row_max)
                if block:
                    expo = jnp.concatenate(
                        [jnp.exp(scores[: extent - TILE] - row_max), expo], axis=0
                    )
                total = jnp.sum(expo, 0, keepdims=True)
                row = pl.multiple_of(pair * 128 + half * 64, 64)
                mixed = dot(vt_ref[pl.ds(row, 64), :extent], expo.astype(BF))
                ctxt_ref[pl.ds(row, 64), columns] = mixed * (1.0 / total)
                lse_ref[pl.ds(pair * 2 + half, 1), columns] = row_max + jnp.log(total)
        turned = pl.ds(pl.multiple_of(pair * 128, 128), 128)
        ctx_ref[:, lanes] = ctxt_ref[turned, :].T.astype(BF)


def attention_forward(own, turn, length, source, gain, shift, bias, pieces):
    slots, model = source.shape
    width = pieces[0].shape[-1]
    outs = []
    if own:
        outs += [out((slots, model), BF), out((model, slots), BF)]
    outs += [out((slots, width), BF)] * 4
    outs += [out((width, slots), F32), out((width // 64, slots), F32)]
    count = len(pieces)
    flops = 2 * slots * model * width * 3 + 2 * slots * slots * width
    return call(
        functools.partial(forward_kernel, own, count),
        "attention_forward_own" if own else "attention_forward_other",
        tuple(outs),
        [smem(), smem()] + [vmem()] * 4 + [anywhere()] * count,
        [
            pltpu.VMEM((3, model, width), BF),
            pltpu.VMEM((width, slots), BF),
            pltpu.VMEM((2, slots, 128), BF),
            pltpu.SemaphoreType.DMA((count,)),
        ],
        flops,
        (turn, length, source, gain, shift, bias, *pieces),
    )


def prepare_kernel(length_ref, cot_ref, gm_ref, gmt_ref, ob_ref):
    slots = cot_ref.shape[0]
    total = jnp.zeros(ob_ref.shape, F32)
    for start in range(0, slots, ROWS):
        rows = slice(start, start + ROWS)
        cot = cot_ref[rows, :].astype(F32)
        position = lax.broadcasted_iota(jnp.int32, cot.shape, 0) + start
        top = jnp.where(position < length_ref[0], cot, 0.0)
        total += jnp.sum(top, 0, keepdims=True)
        low = (BRANCH * top).astype(BF)
        gm_ref[rows, :] = low
        gmt_ref[:, rows] = low.T
    ob_ref[...] = BRANCH * total


def middle_kernel(
    count, turn_ref, x_ref, ctx0_ref, ctx1_ref, proj0_ref, bias_ref, gain_ref, shift_ref, *rest
):
    pieces, rest = rest[:count], rest[count:]
    middle_ref, c_ref, ct_ref, w_ref, sems = rest
    copies = fetch_rows(pieces, w_ref, turn_ref[0], sems)
    for copy in copies:
        copy.start()
    for copy in copies:
        copy.wait()
    slots = x_ref.shape[0]
    for start in range(0, slots, ROWS):
        rows = slice(start, start + ROWS)
        mine = dot(ctx0_ref[rows, :], proj0_ref[...]).astype(BF).astype(F32)
        theirs = dot(ctx1_ref[rows, :], w_ref[...]).astype(BF).astype(F32)
        middle = x_ref[rows, :].astype(F32) + BRANCH * ((mine + theirs) + bias_ref[...])
        middle_ref[rows, :] = middle
        normed, _ = norm_parts(middle)
        low = (normed * gain_ref[...] + shift_ref[...]).astype(BF)
        c_ref[rows, :] = low
        ct_ref[:, rows] = low.T


def mlp_kernel(own, count, turn_ref, c_ref, g_ref, bias_ref, *rest):
    if own:
        ct_ref, gt_ref, rest = rest[0], rest[1], rest[2:]
    fc_pieces, out_pieces, rest = rest[:count], rest[count : 2 * count], rest[2 * count :]
    mlp_ref, gc_ref, rest = rest[0], rest[1], rest[2:]
    if own:
        dwf_ref, dwo_ref, db_ref, rest = rest[0], rest[1], rest[2], rest[3:]
    fc_ref, ow_ref, mlp_acc, gc_acc, act_ref, gh_ref, sems = rest
    copies = fetch_rows(fc_pieces, fc_ref, turn_ref[0], sems.at[0])
    copies += fetch_rows(out_pieces, ow_ref, turn_ref[0], sems.at[1])
    for copy in copies:
        copy.start()
    for copy in copies:
        copy.wait()
    slots = c_ref.shape[0]
    units = fc_ref.shape[1]
    steps = units // HIDDEN

    @pl.loop(0, steps)
    def _(step):
        lanes = pl.ds(pl.multiple_of(step * HIDDEN, HIDDEN), HIDDEN)
        if own:
            total = jnp.zeros((1, HIDDEN), F32)
        for start in range(0, slots, ROWS):
            rows = slice(start, start + ROWS)
            hidden = dot(c_ref[rows, :], fc_ref[:, lanes]) + bias_ref[:, lanes]
            square = hidden * hidden
            tanh = jnp.tanh(hidden * (GELU + GELU * CUBIC * square))
            share = 0.5 + 0.5 * tanh
            value = hidden * share
            slope = share + value * (1.0 - share) * (2.0 * GELU + 6.0 * GELU * CUBIC * square)
            act = value.astype(BF)
            grad = dot_nt(g_ref[rows, :], ow_ref[lanes, :])
            gh = (grad * slope).astype(BF)
            if own:
                act_ref[rows, :] = act
                gh_ref[rows, :] = gh
                total += jnp.sum(gh.astype(F32), 0, keepdims=True)
            mlp_part = dot(act, ow_ref[lanes, :])
            gc_part = dot_nt(gh, fc_ref[:, lanes])

            @pl.when(step == 0)
            def _():
                mlp_acc[rows, :] = mlp_part
                gc_acc[rows, :] = gc_part

            @pl.when(step > 0)
            def _():
                mlp_acc[rows, :] += mlp_part
                gc_acc[rows, :] += gc_part

        if own:
            db_ref[:, lanes] = total
            dwf_ref[:, lanes] = dot(ct_ref[...], gh_ref[...]).astype(BF)
            dwo_ref[:, lanes] = dot(gt_ref[...], act_ref[...]).astype(BF)

    mlp_ref[...] = mlp_acc[...].astype(BF)
    gc_ref[...] = gc_acc[...].astype(BF)


def feed_forward(own, turn, c_low, grad_mlp, bias, c_turned, g_turned, fc_pieces, out_pieces):
    slots, model = c_low.shape
    units = fc_pieces[0].shape[1]
    count = len(fc_pieces)
    outs = [out((slots, model), BF), out((slots, model), BF)]
    args = [turn, c_low, grad_mlp, bias]
    if own:
        outs += [out((model, units), BF), out((model, units), BF), out((1, units), F32)]
        args += [c_turned, g_turned]
    specs = [smem()] + [vmem()] * (len(args) - 1) + [anywhere()] * (2 * count)
    wide = (slots, HIDDEN) if own else (16, 128)
    return call(
        functools.partial(mlp_kernel, own, count),
        "feed_forward_own" if own else "feed_forward_other",
        tuple(outs),
        specs,
        [
            pltpu.VMEM((model, units), BF),
            pltpu.VMEM((units, model), BF),
            pltpu.VMEM((slots, model), F32),
            pltpu.VMEM((slots, model), F32),
            pltpu.VMEM(wide, BF),
            pltpu.VMEM(wide, BF),
            pltpu.SemaphoreType.DMA((2, count)),
        ],
        2 * slots * model * units * (6 if own else 4),
        (*args, *fc_pieces, *out_pieces),
    )


def turn_kernel(
    count,
    turn_ref,
    length_ref,
    middle_ref,
    cot_ref,
    mlp0_ref,
    mlp1_ref,
    gc0_ref,
    gc1_ref,
    gain_ref,
    ob_ref,
    proj0_ref,
    *rest,
):
    pieces, rest = rest[:count], rest[count:]
    y_ref, gmid_ref, ga_ref, do0_ref, do1_ref, sums_ref, w_ref, sems = rest
    copies = fetch_rows(pieces, w_ref, turn_ref[0], sems)
    for copy in copies:
        copy.start()
    for copy in copies:
        copy.wait()
    slots = middle_ref.shape[0]
    gain_sum = jnp.zeros(gain_ref.shape, F32)
    shift_sum = jnp.zeros(gain_ref.shape, F32)
    bias_sum = jnp.zeros(gain_ref.shape, F32)
    for start in range(0, slots, ROWS):
        rows = slice(start, start + ROWS)
        middle = middle_ref[rows, :]
        mlp = mlp0_ref[rows, :].astype(F32) + mlp1_ref[rows, :].astype(F32)
        y_ref[rows, :] = (middle + BRANCH * (mlp + ob_ref[...])).astype(BF)
        grad_c = gc0_ref[rows, :].astype(F32) + gc1_ref[rows, :].astype(F32)
        normed, inverse = norm_parts(middle)
        gain_sum += jnp.sum(grad_c * normed, 0, keepdims=True)
        shift_sum += jnp.sum(grad_c, 0, keepdims=True)
        cot = cot_ref[rows, :].astype(F32)
        position = lax.broadcasted_iota(jnp.int32, cot.shape, 0) + start
        top = jnp.where(position < length_ref[0], cot, 0.0)
        grad_middle = top + norm_back(grad_c, normed, inverse, gain_ref[...])
        bias_sum += jnp.sum(grad_middle, 0, keepdims=True)
        gmid_ref[rows, :] = grad_middle
        low = (BRANCH * grad_middle).astype(BF)
        ga_ref[rows, :] = low
        do0_ref[rows, :] = dot_nt(low, proj0_ref[...]).astype(BF)
        do1_ref[rows, :] = dot_nt(low, w_ref[...]).astype(BF)
    sums_ref[0:1, :] = gain_sum
    sums_ref[1:2, :] = shift_sum
    sums_ref[2:3, :] = BRANCH * bias_sum


def backward_kernel(own, count, turn_ref, length_ref, q_ref, k_ref, v_ref, do_ref, ctxt_ref, lse_ref, *rest):
    if own:
        at_ref, gat_ref, x_ref, rest = rest[0], rest[1], rest[2], rest[3:]
    pieces, rest = rest[:count], rest[count:]
    gin_ref, rest = rest[0], rest[1:]
    if own:
        dw_ref, dp_ref, qvb_ref, sums_ref, rest = rest[0], rest[1], rest[2], rest[3], rest[4:]
    w_ref, dq_ref, dk_ref, dv_ref, dk_acc, dv_acc, aug_ref, kt_ref, delta_ref, sems = rest
    copies = fetch_rows(pieces, w_ref, turn_ref[0], sems)
    for copy in copies:
        copy.start()
    slots, width = q_ref.shape
    length = length_ref[0]

    @pl.loop(0, width // 128)
    def _(pair):
        lanes = pl.ds(pl.multiple_of(pair * 128, 128), 128)
        lane_k = lax.broadcasted_iota(jnp.int32, (slots, 128), 1)
        pos_k = lax.broadcasted_iota(jnp.int32, (slots, 128), 0)
        bias = jnp.where(pos_k < length, 0.0, FILL)
        k_pair = k_ref[:, lanes].astype(F32)
        for half in (0, 1):
            bias_lane = 64 * (1 - half)
            aug_ref[half] = jnp.where(lane_k == bias_lane, bias, k_pair).astype(BF)
        kt_ref[...] = k_ref[:, lanes].T
        product = do_ref[:, lanes].astype(F32).T * ctxt_ref[lanes, :]
        for half in (0, 1):
            delta_ref[half : half + 1, :] = jnp.sum(
                product[64 * half : 64 * half + 64], 0, keepdims=True
            )
        lane_q = lax.broadcasted_iota(jnp.int32, (TILE, 128), 1)
        key_pos = lax.broadcasted_iota(jnp.int32, (TILE, TILE), 0)
        query_pos = lax.broadcasted_iota(jnp.int32, (TILE, TILE), 1)
        causal = jnp.where(key_pos <= query_pos, 0.0, FILL)
        for block in range(slots // TILE):
            columns = slice(block * TILE, (block + 1) * TILE)
            q_pair = q_ref[columns, lanes].astype(F32)
            do_pair = do_ref[columns, lanes].astype(F32)
            q_low, q_aug, do_low, lse, delta = [], [], [], [], []
            for half in (0, 1):
                bias_lane = 64 * (1 - half)
                inside = lane_q // 64 == half
                q_low.append(jnp.where(inside, q_pair, 0.0).astype(BF))
                do_low.append(jnp.where(inside, do_pair, 0.0).astype(BF))
                q_aug.append(
                    jnp.where(inside, q_pair, jnp.where(lane_q == bias_lane, 1.0, 0.0)).astype(BF)
                )
                lse.append(lse_ref[pl.ds(pair * 2 + half, 1), columns])
                delta.append(delta_ref[half : half + 1, columns])
            q_both = jnp.concatenate(q_low, axis=0)
            do_both = jnp.concatenate(do_low, axis=0)
            dqt = [None, None]
            for inner in range(block + 1):
                keys = slice(inner * TILE, (inner + 1) * TILE)
                probs, slopes = [], []
                for half in (0, 1):
                    scores = dot_nt(aug_ref[half, keys, :], q_aug[half])
                    if inner == block:
                        scores = scores + causal
                    prob = jnp.exp(scores - lse[half])
                    grad = dot_nt(v_ref[keys, lanes], do_low[half])
                    slope = (prob * (grad - delta[half])).astype(BF)
                    probs.append(prob.astype(BF))
                    slopes.append(slope)
                    part = dot(kt_ref[64 * half : 64 * half + 64, keys], slope)
                    dqt[half] = part if inner == 0 else dqt[half] + part
                dv_part = dot(jnp.concatenate(probs, axis=1), do_both)
                dk_part = dot(jnp.concatenate(slopes, axis=1), q_both)
                if inner == block:
                    dv_acc[keys, :] = dv_part
                    dk_acc[keys, :] = dk_part
                else:
                    dv_acc[keys, :] += dv_part
                    dk_acc[keys, :] += dk_part
            dq_ref[columns, lanes] = (jnp.concatenate(dqt, axis=0).T * 0.125).astype(BF)
        dk_ref[:, lanes] = dk_acc[...].astype(BF)
        dv_ref[:, lanes] = dv_acc[...].astype(BF)

    for copy in copies:
        copy.wait()
    if own:
        for index, grad_ref in enumerate((dq_ref, dk_ref, dv_ref)):
            dw_ref[index] = dot(at_ref[...], grad_ref[...]).astype(BF)
        qvb_ref[0:1, :] = jnp.sum(dq_ref[...].astype(F32), 0, keepdims=True)
        qvb_ref[1:2, :] = jnp.sum(dv_ref[...].astype(F32), 0, keepdims=True)
        dp_ref[...] = dot(ctxt_ref[...].astype(BF), gat_ref[...]).T.astype(BF)
        gain_sum = jnp.zeros((1, gin_ref.shape[1]), F32)
        shift_sum = jnp.zeros((1, gin_ref.shape[1]), F32)
    for start in range(0, slots, ROWS):
        rows = slice(start, start + ROWS)
        part = dot_nt(dq_ref[rows, :], w_ref[0])
        part += dot_nt(dk_ref[rows, :], w_ref[1])
        part += dot_nt(dv_ref[rows, :], w_ref[2])
        gin_ref[rows, :] = part.astype(BF)
        if own:
            normed, _ = norm_parts(x_ref[rows, :].astype(F32))
            gain_sum += jnp.sum(part * normed, 0, keepdims=True)
            shift_sum += jnp.sum(part, 0, keepdims=True)
    if own:
        sums_ref[0:1, :] = gain_sum
        sums_ref[1:2, :] = shift_sum


def attention_backward(own, turn, length, q, k, v, do, ctxt, lse, extra, pieces):
    slots, width = q.shape
    model = pieces[0].shape[-2] * len(pieces)
    count = len(pieces)
    outs = [out((slots, model), BF)]
    if own:
        outs += [
            out((3, model, width), BF),
            out((model, width), BF),
            out((2, width), F32),
            out((2, model), F32),
        ]
    args = [turn, length, q, k, v, do, ctxt, lse, *extra]
    specs = [smem(), smem()] + [vmem()] * (len(args) - 2) + [anywhere()] * count
    flops = 5 * slots * slots * width + 2 * slots * model * width * (7 if own else 3)
    return call(
        functools.partial(backward_kernel, own, count),
        "attention_backward_own" if own else "attention_backward_other",
        tuple(outs),
        specs,
        [
            pltpu.VMEM((3, model, width), BF),
            pltpu.VMEM((slots, width), BF),
            pltpu.VMEM((slots, width), BF),
            pltpu.VMEM((slots, width), BF),
            pltpu.VMEM((slots, 128), F32),
            pltpu.VMEM((slots, 128), F32),
            pltpu.VMEM((2, slots, 128), BF),
            pltpu.VMEM((128, slots), BF),
            pltpu.VMEM((2, slots), F32),
            pltpu.SemaphoreType.DMA((count,)),
        ],
        flops,
        (*args, *pieces),
    )


def final_kernel(x_ref, gmid_ref, ga0_ref, ga1_ref, gain_ref, gin_ref):
    slots = x_ref.shape[0]
    for start in range(0, slots, ROWS):
        rows = slice(start, start + ROWS)
        normed, inverse = norm_parts(x_ref[rows, :].astype(F32))
        grad_a = ga0_ref[rows, :].astype(F32) + ga1_ref[rows, :].astype(F32)
        gin_ref[rows, :] = gmid_ref[rows, :] + norm_back(grad_a, normed, inverse, gain_ref[...])


def across(value):
    return lax.ppermute(value, "tensor", [(0, 1), (1, 0)])


def swap(value, bit):
    count = lax.axis_size("dp")
    return lax.ppermute(value, "dp", [(i, i ^ bit) for i in range(count)])


def pick(value, index, axis):
    return lax.dynamic_index_in_dim(value, index, axis, keepdims=False)


def split_rows(value, count):
    shape = value.shape
    return value.reshape(*shape[:-2], count, shape[-2] // count, shape[-1])


def halve(total, place, bit):
    pairs = total.reshape(total.shape[0] // 2, 2, *total.shape[1:])
    side = (place // bit) % 2
    return pick(pairs, side, 1), pick(pairs, 1 - side, 1).astype(BF)


def three_parts(value):
    high = lax.reduce_precision(value, 8, 7)
    rest = value - high
    mid = lax.reduce_precision(rest, 8, 7)
    return jnp.concatenate([high, mid, rest - mid], 0).astype(BF)


def two_parts(value):
    high = lax.reduce_precision(value, 8, 7)
    return jnp.concatenate([high, value - high], 0).astype(BF)


def local(
    block_input,
    first_gain,
    first_shift,
    qkv_weight,
    qv_bias,
    proj_weight,
    proj_bias,
    second_gain,
    second_shift,
    fc_weight,
    fc_bias,
    out_weight,
    out_bias,
    cotangent,
    lengths,
):
    slots, model = block_input.shape
    width = qkv_weight.shape[2]
    units = fc_weight.shape[1]
    shards = lax.axis_size("dp")
    place = lax.axis_index("dp")
    quarter = jnp.bitwise_and(place, 3)
    one_bit = jnp.bitwise_and(place, 1)
    turn4 = quarter.reshape(1).astype(jnp.int32)
    turn2 = one_bit.reshape(1).astype(jnp.int32)
    turn0 = jnp.zeros((1,), jnp.int32)
    length = lengths.astype(jnp.int32)
    row = lambda vector: vector.reshape(1, -1)

    biases = jnp.concatenate([qv_bias.reshape(-1), fc_bias]).reshape(-1, model)
    bias_rows = three_parts(biases)
    proj_send = jnp.concatenate([pick(split_rows(proj_weight, 2), one_bit, 0), bias_rows], 0)
    qkv_mine = across(pick(split_rows(qkv_weight, 4), quarter, 1))
    proj_got = across(proj_send)
    fc_mine = across(pick(split_rows(fc_weight, 4), quarter, 0))
    out_mine = across(pick(split_rows(out_weight, 4), quarter, 0))

    def spread(mine):
        side = swap(mine, 2)
        return [mine, swap(mine, 1), side, swap(side, 1)]

    qkv_other = spread(qkv_mine)
    half_rows = width // 2
    proj_mine = proj_got[:half_rows]
    proj_other = [proj_mine, swap(proj_mine, 1)]
    parts = proj_got[half_rows:].astype(F32).reshape(3, -1)
    other_biases = (parts[0] + parts[1]) + parts[2]
    qv_bias_other = other_biases[: 2 * width].reshape(2, width)
    fc_bias_other = other_biases[2 * width :]
    fc_other = spread(fc_mine)
    out_other = spread(out_mine)

    a_low, a_turned, q0, k0, v0, ctx0, ctxt0, lse0 = attention_forward(
        True, turn0, length, block_input, row(first_gain), row(first_shift), qv_bias, [qkv_weight]
    )
    grad_mlp, grad_mlp_turned, grad_out_bias = call(
        prepare_kernel,
        "prepare",
        (out((slots, model), BF), out((model, slots), BF), out((1, model), F32)),
        [smem(), vmem()],
        [],
        8 * slots * model,
        (length, cotangent),
    )
    q1, k1, v1, ctx1, ctxt1, lse1 = attention_forward(
        False, turn4, length, a_low, row(first_gain), row(first_shift), qv_bias_other, qkv_other
    )
    middle, c_low, c_turned = call(
        functools.partial(middle_kernel, 2),
        "middle",
        (out((slots, model), F32), out((slots, model), BF), out((model, slots), BF)),
        [smem()] + [vmem()] * 7 + [anywhere()] * 2,
        [pltpu.VMEM((width, model), BF), pltpu.SemaphoreType.DMA((2,))],
        4 * slots * model * width,
        (
            turn2,
            block_input,
            ctx0,
            ctx1,
            proj_weight,
            row(proj_bias),
            row(second_gain),
            row(second_shift),
            *proj_other,
        ),
    )
    mlp0, gc0, dwf, dwo, grad_fc_bias = feed_forward(
        True, turn0, c_low, grad_mlp, row(fc_bias), c_turned, grad_mlp_turned, [fc_weight], [out_weight]
    )
    mlp1, gc1 = feed_forward(
        False, turn4, c_low, grad_mlp, row(fc_bias_other), None, None, fc_other, out_other
    )

    blocks = jnp.concatenate(
        [dwf.reshape(shards, model // shards, units), dwo.reshape(shards, model // shards, units)], 2
    )
    total = blocks
    bit = 1
    while bit < shards:
        kept, sent = halve(total, place, bit)
        total = kept.astype(F32) + swap(sent, bit).astype(F32)
        bit *= 2
    grad_fc_weight = total[0, :, :units]
    grad_out_weight = total[0, :, units:].T

    block_output, grad_middle, grad_attn, do0, do1, sums2 = call(
        functools.partial(turn_kernel, 2),
        "turn",
        (
            out((slots, model), BF),
            out((slots, model), F32),
            out((slots, model), BF),
            out((slots, width), BF),
            out((slots, width), BF),
            out((3, model), F32),
        ),
        [smem(), smem()] + [vmem()] * 9 + [anywhere()] * 2,
        [pltpu.VMEM((width, model), BF), pltpu.SemaphoreType.DMA((2,))],
        4 * slots * model * width,
        (
            turn2,
            length,
            middle,
            cotangent,
            mlp0,
            mlp1,
            gc0,
            gc1,
            row(second_gain),
            row(out_bias),
            proj_weight,
            *proj_other,
        ),
    )
    ga0, dw, dp, grad_qv, sums1 = attention_backward(
        True,
        turn0,
        length,
        q0,
        k0,
        v0,
        do0,
        ctxt0,
        lse0,
        (a_turned, grad_attn, block_input),
        [qkv_weight],
    )
    (ga1,) = attention_backward(
        False, turn4, length, q1, k1, v1, do1, ctxt1, lse1, (), qkv_other
    )
    (grad_input,) = call(
        final_kernel,
        "final",
        (out((slots, model), F32),),
        [vmem()] * 5,
        [],
        20 * slots * model,
        (block_input, grad_middle, ga0, ga1, row(first_gain)),
    )

    share = model // shards
    blocks = jnp.concatenate(
        [dw[i].reshape(shards, share, width) for i in range(3)] + [dp.reshape(shards, share, width)], 2
    )
    line = 4 * width
    sums1 = sums1 + across(sums1)
    vectors = jnp.concatenate(
        [
            sums1.reshape(-1),
            grad_out_bias.reshape(-1),
            sums2.reshape(-1),
            grad_fc_bias.reshape(-1),
            grad_qv.reshape(-1),
        ]
    )
    used = vectors.shape[0]
    lines = -(-used // line)
    vectors = jnp.pad(vectors, (0, lines * line - used)).reshape(lines, line)
    total = blocks
    bit = 1
    while bit < shards:
        kept, sent = halve(total, place, bit)
        count = sent.shape[0] * share
        sent = jnp.concatenate([sent.reshape(count, line), two_parts(vectors)], 0)
        got = swap(sent, bit).astype(F32)
        total = kept.astype(F32) + got[:count].reshape(kept.shape)
        high = lax.reduce_precision(vectors, 8, 7)
        mine = high + lax.reduce_precision(vectors - high, 8, 7)
        vectors = mine + (got[count : count + lines] + got[count + lines :])
        bit *= 2
    total = total[0]
    grad_qkv_weight = jnp.stack([total[:, i * width : (i + 1) * width] for i in range(3)])
    grad_proj_weight = total[:, 3 * width :].T
    vectors = vectors.reshape(-1)
    sizes = [model] * 6 + [units, 2 * width]
    pieces = []
    start = 0
    for size in sizes:
        pieces.append(vectors[start : start + size])
        start += size
    (
        grad_first_gain,
        grad_first_shift,
        grad_out_bias,
        grad_second_gain,
        grad_second_shift,
        grad_proj_bias,
        grad_fc_bias,
        grad_qv,
    ) = pieces
    return (
        block_output,
        grad_input,
        grad_first_gain,
        grad_first_shift,
        grad_qkv_weight,
        grad_qv.reshape(2, width),
        grad_proj_weight,
        grad_proj_bias,
        grad_second_gain,
        grad_second_shift,
        grad_fc_weight,
        grad_fc_bias,
        grad_out_weight,
        grad_out_bias,
    )


def solution(mesh):
    placed = (
        P("dp", None),
        P(),
        P(),
        P(None, None, "tensor"),
        P(None, "tensor"),
        P("tensor", None),
        P(),
        P(),
        P(),
        P(None, "tensor"),
        P("tensor"),
        P("tensor", None),
        P(),
        P("dp", None),
        P("dp"),
    )
    return jax.shard_map(
        local,
        mesh=mesh,
        in_specs=placed,
        out_specs=(
            P("dp", None),
            P("dp", None),
            P(),
            P(),
            P(None, "dp", "tensor"),
            P(None, "tensor"),
            P("tensor", "dp"),
            P(),
            P(),
            P(),
            P("dp", "tensor"),
            P("tensor"),
            P("tensor", "dp"),
            P(),
        ),
        check_vma=False,
    )
```

time: 720 us -> 294 us (0.41)
  waiting for transfers between devices: 421 us -> 65.6 us
  Pallas kernels: 0 us -> 169 us
  matrix products: 129 us -> 0 us
  blocking collectives: 61.9 us -> 0 us
  other arithmetic: 58.6 us -> 12.1 us
  starting transfers between devices: 1.14 us -> 19.6 us
  between operations: 16.2 us -> 2.31 us
    psum x3 -> x0, waiting for transfers between devices: 192 us -> none  [the longest x1 86.7 us: local(): lax.psum(mlp_part.astype(jnp.bfloat16), 'tensor').astype(jnp.float32)]
    pallas_call x0 -> x10, Pallas kernels: none -> 169 us  [call(): pl.pallas_call(body, name=name, out_shape=outs, in_specs=specs, out_specs...]
    reduce_scatter x3 -> x0, waiting for transfers between devices: 150 us -> none  [the longest x1 79 us: local(): lax.psum_scatter(grad_fc_local, 'dp', scatter_dimension=0, tiled=True)]
    dot_general x18 -> x0, matrix products: 129 us -> none  [the longest x1 16.6 us: attend_back(): jnp.einsum('qhd,khd->hqk', seq_grad, seq_values, preferred_element_type=j...]
    unnamed x8 -> x0, waiting for transfers between devices: 79.4 us -> none
    ppermute x0 -> x23, waiting for transfers between devices: none -> 65.6 us  [the longest x18 60.7 us: swap(): return lax.ppermute(value, 'dp', [(i, i ^ bit) for i in range(count)])]
    psum x1 -> x0, blocking collectives: 61.9 us -> none  [local(): lax.psum((grad_first_gain, grad_first_shift, grad_qv_bias, grad_proj_bias...]
    reduce_sum x10 -> x0, other arithmetic: 30.4 us -> none  [the longest x1 10.3 us: attend(): row_total = jnp.sum(expo, -1, keepdims=True)]
  transfers between devices with their start and end apart: 7 -> 23, of which waited for: 6 -> 10; matrix products, arithmetic and copies ran while one was open for 6% -> 7% of each run, Pallas kernels for 0% -> 38%
where the time goes in v1:
time: 294 us; the launch traced here: 289 us
  Pallas kernels  169 us (57%)
  waiting for transfers between devices  65.6 us (22%)
  local copies, waits for them, and re-layouts  20.6 us (7%)
  starting transfers between devices  19.6 us (7%)
  other arithmetic  12.1 us (4%)
    pallas_call x10, Pallas kernels, call(): pl.pallas_call(body, name=name, out_shape=outs, in_specs=specs, out_specs...  169 us
    ppermute x18, waiting for transfers between devices, swap(): return lax.ppermute(value, 'dp', [(i, i ^ bit) for i in range(count)])  60.7 us
    ppermute x18, starting transfers between devices, swap(): return lax.ppermute(value, 'dp', [(i, i ^ bit) for i in range(count)])  12.7 us
    ppermute x5, starting transfers between devices, across(): return lax.ppermute(value, 'tensor', [(0, 1), (1, 0)])  6.82 us
  transfers between devices with their start and end apart: 23, of which 10 were waited for; matrix products, arithmetic and copies ran while one was open for 7% of the time, Pallas kernels for 38%

profile of v1, /device:TPU:0, one launch (start us, length us, event | category | flops | bytes accessed | tf_op | source)
XLA Modules:
  0.0 288.9 jit_solution(17272846315951715832)
XLA Ops:
  1.9 3.0 %collective-permute-start.1 = (bf16[3,192,384]{2,1,0:T(8,128)(2,1)S(1)}, bf16[3,192,384]{2,1,0:T(8,128)(2,1)}, u32[]{:S(2)}, u32[]{:S(2)}) collective-permute-start(bf16[3,192,384]{2,1,0:T(8,128)(2,1)S(1)} %dynamic-slice_bitcast_fusion.2), channel_id=1, source_target_pairs={{0,1},{1,0},{2,3},{3,2},{4,5},{5,4},{6,7},{7,6},{8,9},{9,8},{10,11... | collective-permute-start | bytes 1327112 | tf_op jit(solution)/shard_map/ppermute | solution.py:525
  7.2 2.1 collective-permute-start.6
  14.2 3.7 %prepare.1 = (bf16[1024,768]{1,0:T(8,128)(2,1)}, bf16[768,1024]{1,0:T(8,128)(2,1)}, f32[1,768]{1,0:T(1,128)}) custom-call(s32[1]{0:T(128)S(6)} %copy.44.length_ref, bf16[1024,768]{1,0:T(8,128)(2,1)} %cot_ref.3), custom_call_target="tpu_custom_call" | custom-call | flops 6291456 | bytes 4721668 | tf_op jit(solution)/shard_map/prepare/pallas_call | solution.py:64
  18.7 2.1 collective-permute-start.3
  20.7 20.4 %attention_forward_own.1 = (bf16[1024,768]{1,0:T(8,128)(2,1)}, bf16[768,1024]{1,0:T(8,128)(2,1)}, bf16[1024,384]{1,0:T(8,128)(2,1)}, bf16[1024,384]{1,0:T(8,128)...) custom-call(s32[1]{0:T(128)} %constant.154.clone.1.turn_ref, ...), custom_call_target="tpu_custom_call" | custom-call | flops 2617245696 | bytes 11240456 | tf_op jit(solution)/shard_map/attention_forward_own/pallas_call | solution.py:64
  41.3 2.1 collective-permute-start.8
  43.3 3.8 %collective-permute-done = bf16[201,768]{1,0:T(8,128)(2,1)S(1)} collective-permute-done((bf16[201,768]{1,0:T(8,128)(2,1)S(1)}, bf16[201,768]{1,0:T(8,128)(2,1)S(1)}, u32[]{:S(2)}, u32[]{:S(2)}) %collective-permute-start) | collective-permute-done | bytes 308768 | tf_op jit(solution)/shard_map/ppermute | solution.py:525
  49.5 7.9 %collective-permute-done.12.rest_6_ = bf16[384,768]{1,0:T(8,128)(2,1)S(1)} collective-permute-done((bf16[384,768]{1,0:T(8,128)(2,1)S(1)}, bf16[384,768]{1,0:T(8,128)(2,1)S(1)}, u32[]{:S(2)}, u32[]{:S(2)}) %collective-permute-start.12) | collective-permute-done | bytes 589856 | tf_op jit(solution)/shard_map/ppermute | solution.py:530
  57.5 10.1 %collective-permute-done.8.rest_2_ = bf16[192,1536]{1,0:T(8,128)(2,1)} collective-permute-done((bf16[192,1536]{1,0:T(8,128)(2,1)}, bf16[192,1536]{1,0:T(8,128)(2,1)}, u32[]{:S(2)}, u32[]{:S(2)}) %collective-permute-start.8) | collective-permute-done | bytes 589856 | tf_op jit(solution)/shard_map/ppermute | solution.py:530
  68.1 19.7 %attention_forward_other.1 = (bf16[1024,384]{1,0:T(8,128)(2,1)}, bf16[1024,384]{1,0:T(8,128)(2,1)}, bf16[1024,384]{1,0:T(8,128)(2,1)}, bf16[1024,384]{1,0:T(8,12...) custom-call(s32[1]{0:T(128)} %bitcast.1.turn_ref, s32[1]{0:T(128)S(6)} %copy.44.length_ref, ...), custom_call_target="tpu_custom_call" | custom-call | flops 2617245696 | bytes 8094728 | tf_op jit(solution)/shard_map/attention_forward_other/pallas_call | solution.py:64
  88.6 8.2 %middle.1 = (f32[1024,768]{1,0:T(8,128)}, bf16[1024,768]{1,0:T(8,128)(2,1)}, bf16[768,1024]{1,0:T(8,128)(2,1)}) custom-call(s32[1]{0:T(128)} %bitcast.turn_ref, bf16[1024,768]{1,0:T(8,128)(2,1)} %x_ref.3, bf16[1024,384]{1,0:T(8,128)(2,1)} %get-tuple-element.52.ctx0_ref, bf16[1024,384]{1,0:T(8,128)(2,1)} %get-tuple-element.54.ctx1_ref, ...), custom_call_target="tpu_custom_call" | custom-call | flops 1207959552 | bytes 10626052 | tf_op jit(solution)/shard_map/middle/pallas_call | solution.py:64
  96.9 27.5 %feed_forward_own.1 = (bf16[1024,768]{1,0:T(8,128)(2,1)}, bf16[1024,768]{1,0:T(8,128)(2,1)}, bf16[768,1536]{1,0:T(8,128)(2,1)}, bf16[768,1536]{1,0:T(8,128)(2,1)}, f32[1,1536]{1,0:T(1,128)}) custom-call(s32[1]{0:T(128)} %constant.154.clone.1.turn_ref, bf16[1024,768]{1,0:T(8,128)(2,1)} %get-tuple-element.56.c_ref, bf16[1024,768]{1,0:T(8,128)(2,1)} %get-tuple-element.57.g_ref, ...), custom_call_target="tpu_custom_call" | custom-call | flops 14495514624 | bytes 18886660 | tf_op jit(solution)/shard_map/feed_forward_own/pallas_call | solution.py:64
  126.2 19.1 %feed_forward_other.1 = (bf16[1024,768]{1,0:T(8,128)(2,1)}, bf16[1024,768]{1,0:T(8,128)(2,1)}) custom-call(s32[1]{0:T(128)} %bitcast.1.turn_ref, bf16[1024,768]{1,0:T(8,128)(2,1)} %get-tuple-element.56.c_ref, bf16[1024,768]{1,0:T(8,128)(2,1)} %get-tuple-element.57.g_ref, f32[1,1536]{1,0:T(1,128)} %bitcast.104, ...), custom_call_target="tpu_custom_call" | custom-call | flops 9663676416 | bytes 11016196 | tf_op jit(solution)/shard_map/feed_forward_other/pallas_call | solution.py:64
  145.3 12.4 %turn.1 = (bf16[1024,768]{1,0:T(8,128)(2,1)}, f32[1024,768]{1,0:T(8,128)}, bf16[1024,768]{1,0:T(8,128)(2,1)}, bf16[1024,384]{1,0:T(8,128)(2,1)}, bf16[1024,384]{1,0:T(8,128)(2,1)}, /*index=5*/f32[3,768]{1,0:T(4,128)}) custom-call(s32[1]{0:T(128)} %bitcast.turn_ref, s32[1]{0:T(128)S(6)} %copy.44.length_ref, f32[1024,768]{1,0:T(8,128)} %get-tuple-element.55.middle_ref, ...), custom_call_target="tpu_custom_call" | custom-call | flops 1207959552 | bytes 20069384 | tf_op jit(solution)/shard_map/turn/pallas_call | solution.py:64
  157.7 27.6 %attention_backward_own.1 = (bf16[1024,768]{1,0:T(8,128)(2,1)}, bf16[3,768,384]{2,1,0:T(8,128)(2,1)}, bf16[768,384]{1,0:T(8,128)(2,1)}, f32[2,384]{1,0:T(2,128)}, f32[2,768]{1,0:T(2,128)}) custom-call(s32[1]{0:T(128)} %constant.154.clone.1.turn_ref, s32[1]{0:T(128)S(6)} %copy.44.length_ref, bf16[1024,384]{1,0:T(8,128)(2,1)} %get-tuple-element.66.q_ref, ...), custom_call_target="tpu_custom_call" | custom-call | flops 6241124352 | bytes 15172616 | tf_op jit(solution)/shard_map/attention_backward_own/pallas_call | solution.py:64
  185.3 1.7 fusion.19
  187.0 1.6 collective-permute-start.14
  192.0 3.1 %collective-permute-done.15 = bf16[394,1536]{1,0:T(8,128)(2,1)S(1)} collective-permute-done((bf16[394,1536]{1,0:T(8,128)(2,1)}, bf16[394,1536]{1,0:T(8,128)(2,1)S(1)}, u32[]{:S(2)}, u32[]{:S(2)}) %collective-permute-start.15) | collective-permute-done | bytes 1210400 | tf_op jit(solution)/shard_map/ppermute | solution.py:530
  196.1 1.4 copy-done.4
  199.6 1.8 fusion.1
  201.5 1.3 constant_dynamic-slice_fusion
  202.8 12.3 %collective-permute-done.16 = bf16[202,1536]{1,0:T(8,128)(2,1)S(1)} collective-permute-done((bf16[202,1536]{1,0:T(8,128)(2,1)}, bf16[202,1536]{1,0:T(8,128)(2,1)S(1)}, u32[]{:S(2)}, u32[]{:S(2)}) %collective-permute-start.16) | collective-permute-done | bytes 620576 | tf_op jit(solution)/shard_map/ppermute | solution.py:530
  215.7 1.6 collective-permute-start.17
  217.3 2.4 convert_add_fusion
  220.5 4.6 %collective-permute-done.17 = bf16[106,1536]{1,0:T(8,128)(2,1)S(1)} collective-permute-done((bf16[106,1536]{1,0:T(8,128)(2,1)S(1)}, bf16[106,1536]{1,0:T(8,128)(2,1)S(1)}, u32[]{:S(2)}, u32[]{:S(2)}) %collective-permute-start.17) | collective-permute-done | bytes 325664 | tf_op jit(solution)/shard_map/ppermute | solution.py:530
  225.3 2.7 collective-permute-start.18
  228.0 22.9 %attention_backward_other.1.ga1_ref = bf16[1024,768]{1,0:T(8,128)(2,1)} custom-call(s32[1]{0:T(128)} %bitcast.1.turn_ref, s32[1]{0:T(128)S(6)} %copy.44.length_ref, bf16[1024,384]{1,0:T(8,128)(2,1)} %get-tuple-element.75.q_ref, bf16[1024,384]{1,0:T(8,128)(2,1)} %get-tuple-element.76.k_ref, bf16[1024,384]{1,0:T(8,128)(2,1)} %get-tuple-element.77.v_ref, ...), custom_call_target="tpu_custom_call" | custom-call | flops 3825205248 | bytes 8085512 | tf_op jit(solution)/shard_map/attention_backward_other/pallas_call | solution.py:64
  250.9 7.1 %final.1 = f32[1024,768]{1,0:T(8,128)} custom-call(bf16[1024,768]{1,0:T(8,128)(2,1)} %x_ref.3, f32[1024,768]{1,0:T(8,128)} %get-tuple-element.65.gmid_ref, bf16[1024,768]{1,0:T(8,128)(2,1)} %get-tuple-element.74.ga0_ref, bf16[1024,768]{1,0:T(8,128)(2,1)} %attention_backward_other.1.ga1_ref, f32[1,768]{1,0:T(1,128)} %reshape.200.gain_ref), custom_call_target="tpu_custom_call" | custom-call | flops 15728640 | bytes 11013120 | tf_op jit(solution)/shard_map/final/pallas_call | solution.py:64
  258.8 1.9 bitcast_add_fusion
  260.8 1.6 collective-permute-start.21
  263.8 10.6 %collective-permute-done.21 = bf16[2,48,3072]{2,1,0:T(8,128)(2,1)S(1)} collective-permute-done((bf16[2,48,3072]{2,1,0:T(8,128)(2,1)S(1)}, bf16[2,48,3072]{2,1,0:T(8,128)(2,1)S(1)}, u32[]{:S(2)}, u32[]{:S(2)}) %collective-permute-start.21) | collective-permute-done | bytes 589856 | tf_op jit(solution)/shard_map/ppermute | solution.py:530
  276.0 11.7 %collective-permute-done.22 = bf16[1,48,3072]{2,1,0:T(8,128)(2,1)S(1)} collective-permute-done((bf16[1,48,3072]{2,1,0:T(8,128)(2,1)S(1)}, bf16[1,48,3072]{2,1,0:T(8,128)(2,1)S(1)}, u32[]{:S(2)}, u32[]{:S(2)}) %collective-permute-start.22) | collective-permute-done | bytes 294944 | tf_op jit(solution)/shard_map/ppermute | solution.py:530
  (155 shorter events, 26.3 us)
Async XLA Ops:
  0.7 10.1 %copy-start.12 = (f32[768]{0:T(1024)S(1)}, f32[768]{0:T(1024)}, u32[]{:S(2)}) copy-start(f32[768]{0:T(1024)} %param.16) | copy-start | bytes 9220
  0.7 10.6 %copy-start.13 = (f32[768]{0:T(1024)S(1)}, f32[768]{0:T(1024)}, u32[]{:S(2)}) copy-start(f32[768]{0:T(1024)} %param.17) | copy-start | bytes 9220
  0.7 11.2 %copy-start.14 = (f32[768]{0:T(1024)S(1)}, f32[768]{0:T(1024)}, u32[]{:S(2)}) copy-start(f32[768]{0:T(1024)} %param.22) | copy-start | bytes 9220
  0.7 11.8 %copy-start.15 = (f32[768]{0:T(1024)S(1)}, f32[768]{0:T(1024)}, u32[]{:S(2)}) copy-start(f32[768]{0:T(1024)} %param.21) | copy-start | bytes 9220
  0.7 12.4 %copy-start.16 = (f32[768]{0:T(1024)S(1)}, f32[768]{0:T(1024)}, u32[]{:S(2)}) copy-start(f32[768]{0:T(1024)} %param.23) | copy-start | bytes 9220
  0.7 12.9 %copy-start.17 = (f32[768]{0:T(1024)S(1)}, f32[768]{0:T(1024)}, u32[]{:S(2)}) copy-start(f32[768]{0:T(1024)} %param.27) | copy-start | bytes 9220
  1.9 16.8 %collective-permute-start.1 = (bf16[3,192,384]{2,1,0:T(8,128)(2,1)S(1)}, bf16[3,192,384]{2,1,0:T(8,128)(2,1)}, u32[]{:S(2)}, u32[]{:S(2)}) collective-permute-start(bf16[3,192,384]{2,1,0:T(8,128)(2,1)S(1)} %dynamic-slice_bitcast_fusion.2), channel_id=1, source_target_pairs={{0,1},{1,0},{2,3},{3,2},{4,5},{5,4},{6,7},{7,6},{8,9},{9,8},{10,11... | collective-permute-start | bytes 1327112 | tf_op jit(solution)/shard_map/ppermute | solution.py:525
  6.0 35.1 %collective-permute-start.10 = (bf16[384,768]{1,0:T(8,128)(2,1)S(1)}, bf16[384,768]{1,0:T(8,128)(2,1)S(1)}, u32[]{:S(2)}, u32[]{:S(2)}) collective-permute-start(bf16[384,768]{1,0:T(8,128)(2,1)S(1)} %dynamic-slice_bitcast_fusion), channel_id=1, source_target_pairs={{0,1},{1,0},{2,3},{3,2},{4,5},{5,4},{6,7},{7,6},{8,9},{9,8},{10,11... | collective-permute-start | bytes 1769480 | tf_op jit(solution)/shard_map/ppermute | solution.py:525
  7.2 34.1 %collective-permute-start.6 = (bf16[192,1536]{1,0:T(8,128)(2,1)S(1)}, bf16[192,1536]{1,0:T(8,128)(2,1)}, u32[]{:S(2)}, u32[]{:S(2)}) collective-permute-start(bf16[192,1536]{1,0:T(8,128)(2,1)S(1)} %dynamic-slice_bitcast_fusion.1), channel_id=1, source_target_pairs={{0,1},{1,0},{2,3},{3,2},{4,5},{5,4},{6,7},{7,6},{8,9},{9,8},{10,11... | collective-permute-start | bytes 1769480 | tf_op jit(solution)/shard_map/ppermute | solution.py:525
  9.4 37.8 %collective-permute-start = (bf16[201,768]{1,0:T(8,128)(2,1)S(1)}, bf16[201,768]{1,0:T(8,128)(2,1)S(1)}, u32[]{:S(2)}, u32[]{:S(2)}) collective-permute-start(bf16[201,768]{1,0:T(8,128)(2,1)S(1)} %pad_maximum_fusion.4), channel_id=1, source_target_pairs={{0,1},{1,0},{2,3},{3,2},{4,5},{5,4},{6,7},{7,6},{8,9},{9,8},{10,11... | collective-permute-start | bytes 926216 | tf_op jit(solution)/shard_map/ppermute | solution.py:525
  18.7 28.5 %collective-permute-start.3 = (bf16[3,192,384]{2,1,0:T(8,128)(2,1)}, bf16[3,192,384]{2,1,0:T(8,128)(2,1)}, u32[]{:S(2)}, u32[]{:S(2)}) collective-permute-start(bf16[3,192,384]{2,1,0:T(8,128)(2,1)} %collective-permute-done.1.rest_0_), channel_id=1, source_target_pairs={{0,4},{2,6},{4,0},{6,2},{8,12},{10,14},{12,8},{14,10},{16,20},{18,... | collective-permute-start | bytes 1327112 | tf_op jit(solution)/shard_map/ppermute | solution.py:530
  41.1 46.7 %copy-start.20 = (bf16[384,768]{1,0:T(8,128)(2,1)}, bf16[384,768]{1,0:T(8,128)(2,1)S(1)}, u32[]{:S(2)}) copy-start(bf16[384,768]{1,0:T(8,128)(2,1)S(1)} %collective-permute-done.10.rest_4_) | copy-start | bytes 1769476
  41.1 16.3 %collective-permute-start.12 = (bf16[384,768]{1,0:T(8,128)(2,1)S(1)}, bf16[384,768]{1,0:T(8,128)(2,1)S(1)}, u32[]{:S(2)}, u32[]{:S(2)}) collective-permute-start(bf16[384,768]{1,0:T(8,128)(2,1)S(1)} %collective-permute-done.10.rest_4_), channel_id=1, source_target_pairs={{0,4},{2,6},{4,0},{6,2},{8,12},{10,14},{12,8},{14,10},{16,20},{18,... | collective-permute-start | bytes 1769480 | tf_op jit(solution)/shard_map/ppermute | solution.py:530
  41.3 26.4 %collective-permute-start.8 = (bf16[192,1536]{1,0:T(8,128)(2,1)}, bf16[192,1536]{1,0:T(8,128)(2,1)}, u32[]{:S(2)}, u32[]{:S(2)}) collective-permute-start(bf16[192,1536]{1,0:T(8,128)(2,1)} %collective-permute-done.6.rest_0_), channel_id=1, source_target_pairs={{0,4},{2,6},{4,0},{6,2},{8,12},{10,14},{12,8},{14,10},{16,20},{18,... | collective-permute-start | bytes 1769480 | tf_op jit(solution)/shard_map/ppermute | solution.py:530
  47.2 2.1 collective-permute-start.2
  47.2 20.4 %collective-permute-start.4 = (bf16[3,192,384]{2,1,0:T(8,128)(2,1)}, bf16[3,192,384]{2,1,0:T(8,128)(2,1)}, u32[]{:S(2)}, u32[]{:S(2)}) collective-permute-start(bf16[3,192,384]{2,1,0:T(8,128)(2,1)} %collective-permute-done.3.rest_2_), channel_id=1, source_target_pairs={{0,2},{2,0},{4,6},{6,4},{8,10},{10,8},{12,14},{14,12},{16,18},{18,... | collective-permute-start | bytes 1327112 | tf_op jit(solution)/shard_map/ppermute | solution.py:530
  47.7 40.1 %copy-start.6 = (bf16[192,768]{1,0:T(8,128)(2,1)}, bf16[192,768]{1,0:T(8,128)(2,1)S(1)}, u32[]{:S(2)}) copy-start(bf16[192,768]{1,0:T(8,128)(2,1)S(1)} %slice.166.rest_0_) | copy-start | bytes 884740
  47.7 40.1 %collective-permute-start.5 = (bf16[192,768]{1,0:T(8,128)(2,1)S(1)}, bf16[192,768]{1,0:T(8,128)(2,1)S(1)}, u32[]{:S(2)}, u32[]{:S(2)}) collective-permute-start(bf16[192,768]{1,0:T(8,128)(2,1)S(1)} %slice.166.rest_0_), channel_id=1, source_target_pairs={{0,2},{2,0},{4,6},{6,4},{8,10},{10,8},{12,14},{14,12},{16,18},{18,... | collective-permute-start | bytes 884744 | tf_op jit(solution)/shard_map/ppermute | solution.py:530
  49.3 75.8 %collective-permute-start.11 = (bf16[384,768]{1,0:T(8,128)(2,1)S(1)}, bf16[384,768]{1,0:T(8,128)(2,1)S(1)}, u32[]{:S(2)}, u32[]{:S(2)}) collective-permute-start(bf16[384,768]{1,0:T(8,128)(2,1)S(1)} %collective-permute-done.10.rest_4_), channel_id=1, source_target_pairs={{0,2},{2,0},{4,6},{6,4},{8,10},{10,8},{12,14},{14,12},{16,18},{18,... | collective-permute-start | bytes 1769480 | tf_op jit(solution)/shard_map/ppermute | solution.py:530
  57.5 30.4 %copy-start.21 = (bf16[384,768]{1,0:T(8,128)(2,1)}, bf16[384,768]{1,0:T(8,128)(2,1)S(1)}, u32[]{:S(2)}) copy-start(bf16[384,768]{1,0:T(8,128)(2,1)S(1)} %collective-permute-done.12.rest_6_) | copy-start | bytes 1769476
  57.5 67.7 %collective-permute-start.7 = (bf16[192,1536]{1,0:T(8,128)(2,1)}, bf16[192,1536]{1,0:T(8,128)(2,1)S(1)}, u32[]{:S(2)}, u32[]{:S(2)}) collective-permute-start(bf16[192,1536]{1,0:T(8,128)(2,1)} %collective-permute-done.6.rest_0_), channel_id=1, source_target_pairs={{0,2},{2,0},{4,6},{6,4},{8,10},{10,8},{12,14},{14,12},{16,18},{18,... | collective-permute-start | bytes 1769480 | tf_op jit(solution)/shard_map/ppermute | solution.py:530
  67.6 57.5 %collective-permute-start.13 = (bf16[384,768]{1,0:T(8,128)(2,1)S(1)}, bf16[384,768]{1,0:T(8,128)(2,1)}, u32[]{:S(2)}, u32[]{:S(2)}) collective-permute-start(bf16[384,768]{1,0:T(8,128)(2,1)S(1)} %collective-permute-done.12.rest_6_), channel_id=1, source_target_pairs={{0,2},{2,0},{4,6},{6,4},{8,10},{10,8},{12,14},{14,12},{16,18},{18,... | collective-permute-start | bytes 1769480 | tf_op jit(solution)/shard_map/ppermute | solution.py:530
  67.6 57.5 %collective-permute-start.9 = (bf16[192,1536]{1,0:T(8,128)(2,1)}, bf16[192,1536]{1,0:T(8,128)(2,1)}, u32[]{:S(2)}, u32[]{:S(2)}) collective-permute-start(bf16[192,1536]{1,0:T(8,128)(2,1)} %collective-permute-done.8.rest_2_), channel_id=1, source_target_pairs={{0,2},{2,0},{4,6},{6,4},{8,10},{10,8},{12,14},{14,12},{16,18},{18,... | collective-permute-start | bytes 1769480 | tf_op jit(solution)/shard_map/ppermute | solution.py:530
  187.0 3.7 %collective-permute-start.14 = (f32[2,768]{1,0:T(2,128)S(1)}, f32[2,768]{1,0:T(2,128)S(1)}, u32[]{:S(2)}, u32[]{:S(2)}) collective-permute-start(f32[2,768]{1,0:T(2,128)S(1)} %copy-done.11), channel_id=1, source_target_pairs={{0,1},{1,0},{2,3},{3,2},{4,5},{5,4},{6,7},{7,6},{8,9},{9,8},{10,11... | collective-permute-start | bytes 18440 | tf_op jit(solution)/shard_map/ppermute | solution.py:525
  192.0 3.1 %collective-permute-start.15 = (bf16[394,1536]{1,0:T(8,128)(2,1)}, bf16[394,1536]{1,0:T(8,128)(2,1)S(1)}, u32[]{:S(2)}, u32[]{:S(2)}) collective-permute-start(bf16[394,1536]{1,0:T(8,128)(2,1)} %pad_maximum_fusion.1), channel_id=1, source_target_pairs={{0,2},{2,0},{4,6},{6,4},{8,10},{10,8},{12,14},{14,12},{16,18},{18,... | collective-permute-start | bytes 3631112 | tf_op jit(solution)/shard_map/ppermute | solution.py:530
  198.5 16.6 %collective-permute-start.16 = (bf16[202,1536]{1,0:T(8,128)(2,1)}, bf16[202,1536]{1,0:T(8,128)(2,1)S(1)}, u32[]{:S(2)}, u32[]{:S(2)}) collective-permute-start(bf16[202,1536]{1,0:T(8,128)(2,1)} %pad_maximum_fusion.2), channel_id=1, source_target_pairs={{0,4},{2,6},{4,0},{6,2},{8,12},{10,14},{12,8},{14,10},{16,20},{18,... | collective-permute-start | bytes 1861640 | tf_op jit(solution)/shard_map/ppermute | solution.py:530
  201.4 16.0 %collective-permute-start.19 = (bf16[8,48,3072]{2,1,0:T(8,128)(2,1)}, bf16[8,48,3072]{2,1,0:T(8,128)(2,1)}, u32[]{:S(2)}, u32[]{:S(2)}) collective-permute-start(bf16[8,48,3072]{2,1,0:T(8,128)(2,1)} %fusion.1), channel_id=1, source_target_pairs={{0,2},{2,0},{4,6},{6,4},{8,10},{10,8},{12,14},{14,12},{16,18},{18,... | collective-permute-start | bytes 7077896 | tf_op jit(solution)/shard_map/ppermute | solution.py:530
  215.7 9.3 %collective-permute-start.17 = (bf16[106,1536]{1,0:T(8,128)(2,1)S(1)}, bf16[106,1536]{1,0:T(8,128)(2,1)S(1)}, u32[]{:S(2)}, u32[]{:S(2)}) collective-permute-start(bf16[106,1536]{1,0:T(8,128)(2,1)S(1)} %pad_maximum_fusion.3), channel_id=1, source_target_pairs={{0,8},{2,10},{4,12},{6,14},{8,0},{10,2},{12,4},{14,6},{16,24},{18,... | collective-permute-start | bytes 976904 | tf_op jit(solution)/shard_map/ppermute | solution.py:530
  219.9 38.9 %collective-permute-start.20 = (bf16[4,48,3072]{2,1,0:T(8,128)(2,1)S(1)}, bf16[4,48,3072]{2,1,0:T(8,128)(2,1)S(1)}, u32[]{:S(2)}, u32[]{:S(2)}) collective-permute-start(bf16[4,48,3072]{2,1,0:T(8,128)(2,1)S(1)} %fusion.4), channel_id=1, source_target_pairs={{0,4},{2,6},{4,0},{6,2},{8,12},{10,14},{12,8},{14,10},{16,20},{18,... | collective-permute-start | bytes 3538952 | tf_op jit(solution)/shard_map/ppermute | solution.py:530
  225.3 32.7 %collective-permute-start.18 = (bf16[58,1536]{1,0:T(8,128)(2,1)S(1)}, bf16[58,1536]{1,0:T(8,128)(2,1)S(1)}, u32[]{:S(2)}, u32[]{:S(2)}) collective-permute-start(bf16[58,1536]{1,0:T(8,128)(2,1)S(1)} %pad_maximum_fusion.6), channel_id=1, source_target_pairs={{0,16},{2,18},{4,20},{6,22},{8,24},{10,26},{12,28},{14,30},{16,0},... | collective-permute-start | bytes 534536 | tf_op jit(solution)/shard_map/ppermute | solution.py:530
  260.8 13.6 %collective-permute-start.21 = (bf16[2,48,3072]{2,1,0:T(8,128)(2,1)S(1)}, bf16[2,48,3072]{2,1,0:T(8,128)(2,1)S(1)}, u32[]{:S(2)}, u32[]{:S(2)}) collective-permute-start(bf16[2,48,3072]{2,1,0:T(8,128)(2,1)S(1)} %fusion.5), channel_id=1, source_target_pairs={{0,8},{2,10},{4,12},{6,14},{8,0},{10,2},{12,4},{14,6},{16,24},{18,... | collective-permute-start | bytes 1769480 | tf_op jit(solution)/shard_map/ppermute | solution.py:530
  274.6 13.1 %collective-permute-start.22 = (bf16[1,48,3072]{2,1,0:T(8,128)(2,1)S(1)}, bf16[1,48,3072]{2,1,0:T(8,128)(2,1)S(1)}, u32[]{:S(2)}, u32[]{:S(2)}) collective-permute-start(bf16[1,48,3072]{2,1,0:T(8,128)(2,1)S(1)} %dynamic-slice_convert_fusion.3), channel_id=1, source_target_pairs={{0,16},{2,18},{4,20},{6,22},{8,24},{10,26},{12,28},{14,30},{16,0},... | collective-permute-start | bytes 884744 | tf_op jit(solution)/shard_map/ppermute | solution.py:530
  (15 other events, 48.7 us)
